TPU v7x, 32 devices: a whole 2x2x4 slice. The times are simulated.
32 devices in a mesh: grp: 4 (over x, core), tp: 4 (over z), cores: 2 (over y).
Axes of the slice: x: 2, y: 2, z: 4, core: 2. Of those that a mesh axis runs over, the one named last changes fastest.
Arguments:
- tokens: bfloat16 [4096, 8192], P('grp', ('tp', 'cores')), may hold values from -6 to 6
- gate_up_weight: bfloat16 [8192, 2, 16384], P(None, None, ('tp', 'cores')), may hold values from -0.0625 to 0.0625
- down_factor_pool: bfloat16 [8, 8192, 256], P(('tp', 'cores'), 'grp'), may hold values from -0.0625 to 0.0625
- up_factor_pool: bfloat16 [8, 4, 8, 128, 1024], P(('tp', 'cores'), 'grp'), may hold values from -0.5 to 0.5
- segment_adapters: int32 [4, 3], replicated, may hold values from 0 to 7
- segment_tile_counts: int32 [4, 3], P('grp'), may hold values from 1 to 4, 8 in all within a row
- adapter_pool_rows: int32 [8], replicated, may hold values from 0 to 7, each once
Outputs:
- hidden: bfloat16 [4096, 16384], P('grp', ('tp', 'cores'))
Inputs may be any that keep to these rules, and one draw needn't show every extreme that they name: `segment_tile_counts`: each row sums to 8. `adapter_pool_rows`: each pool row appears once.
All inputs are finite; a program needn't handle non-finite values.
Results may differ from a plain program's by a relative error of at most 0.0036.
Values may be sent and summed in bfloat16 or wider, within the bound.
A program may use at most 320 MiB of HBM per device.

v0:
```python
import jax
import jax.numpy as jnp
from jax import lax
from jax.sharding import PartitionSpec as P

TILE = 128
adapter_scale = 0.5


def tile_segments(tile_lengths, tile_count):
    bounds = jnp.cumsum(tile_lengths)
    positions = jnp.arange(tile_count, dtype=jnp.int32)
    return jnp.sum((bounds[None, :] <= positions[:, None]).astype(jnp.int32), axis=1)


def per_device(
    tokens,
    gate_up_weight,
    down_factor_pool,
    up_factor_pool,
    segment_adapters,
    segment_tile_counts,
    adapter_pool_rows,
):
    groups = lax.axis_size("grp")
    device_shares = lax.axis_size(("tp", "cores"))
    piece_index = lax.axis_index(("tp", "cores"))
    token_count = tokens.shape[0]
    full_width = tokens.shape[1] * device_shares
    local_hidden_width = gate_up_weight.shape[2]
    twice_rank = down_factor_pool.shape[2]
    rank_size = twice_rank // 2
    share_rows = down_factor_pool.shape[1] // device_shares
    local_count = down_factor_pool.shape[0]
    seg_count = segment_adapters.shape[1]
    narrow = local_hidden_width // groups
    local_down_factor = down_factor_pool.reshape(
        local_count, device_shares, share_rows * twice_rank
    )
    local_up_factor = up_factor_pool.reshape(local_count, device_shares, -1)
    a_spread, b_spread = (
        lax.all_to_all(local_down_factor, ("tp", "cores"), split_axis=1, concat_axis=0, tiled=True),
        lax.all_to_all(local_up_factor, ("tp", "cores"), split_axis=1, concat_axis=0, tiled=True),
    )
    all_slots = jnp.take(adapter_pool_rows, segment_adapters)
    a_wanted = jnp.take(a_spread, all_slots, axis=0)
    b_wanted = jnp.take(b_spread, all_slots, axis=0)
    a_arrived, b_arrived = (
        lax.all_to_all(a_wanted, "grp", split_axis=0, concat_axis=2, tiled=True),
        lax.all_to_all(b_wanted, "grp", split_axis=0, concat_axis=2, tiled=True),
    )
    a_chosen = a_arrived.reshape(seg_count, groups, -1)
    b_chosen = b_arrived.reshape(seg_count, groups, -1)
    gathered = lax.all_gather(tokens, ("tp", "cores"), axis=1, tiled=True)
    frozen_output = jnp.dot(
        gathered,
        gate_up_weight.reshape(full_width, 2 * local_hidden_width),
        preferred_element_type=jnp.float32,
    )
    frozen_output = frozen_output.reshape(token_count, 2, local_hidden_width)
    tile_count = token_count // TILE
    tile_seg = tile_segments(segment_tile_counts[0], tile_count)
    a_tiles = jnp.take(a_chosen, tile_seg, axis=0).reshape(
        tile_count, groups * share_rows, twice_rank
    )
    own_features = lax.dynamic_slice_in_dim(
        gathered.reshape(token_count, groups, device_shares, share_rows), piece_index, 1, axis=2
    )
    own_features = own_features.reshape(tile_count, TILE, groups * share_rows)
    partial_shrink = jnp.einsum(
        "tkd,tdr->tkr", own_features, a_tiles, preferred_element_type=jnp.float32
    )
    reduced_input = lax.psum(partial_shrink, ("tp", "cores")).astype(jnp.bfloat16)
    b_tiles = jnp.take(b_chosen, tile_seg, axis=0).reshape(tile_count, groups, rank_size, 2, narrow)
    gate_adapter_delta = jnp.einsum(
        "tkr,tmrw->tkmw",
        reduced_input[:, :, :rank_size],
        b_tiles[:, :, :, 0, :],
        preferred_element_type=jnp.float32,
    )
    up_adapter_delta = jnp.einsum(
        "tkr,tmrw->tkmw",
        reduced_input[:, :, rank_size:],
        b_tiles[:, :, :, 1, :],
        preferred_element_type=jnp.float32,
    )
    gate_combined = frozen_output[:, 0, :] + adapter_scale * gate_adapter_delta.reshape(
        token_count, local_hidden_width
    )
    up_combined = frozen_output[:, 1, :] + adapter_scale * up_adapter_delta.reshape(
        token_count, local_hidden_width
    )
    return (jax.nn.silu(gate_combined) * up_combined).astype(jnp.bfloat16)


def solution(mesh):
    return jax.shard_map(
        per_device,
        mesh=mesh,
        in_specs=(
            P("grp", ("tp", "cores")),
            P(None, None, ("tp", "cores")),
            P(("tp", "cores"), "grp", None),
            P(("tp", "cores"), "grp", None, None, None),
            P(),
            P("grp", None),
            P(),
        ),
        out_specs=P("grp", ("tp", "cores")),
        check_vma=False,
    )
```

profile of v0, /device:TPU:0, one launch (start us, length us, event | category | flops | bytes accessed | tf_op | source)
XLA Modules:
  0.0 634.1 jit_solution(12954752661760870075)
XLA Ops:
  11.1 7.3 %reduce.3 = bf16[8,65536]{1,0:T(8,128)(2,1)S(1)} reduce(bf16[8,1,65536]{2,1,0:T(2,128)(2,1)S(1)} %bitcast.106, bf16[]{:T(256)} %broadcast.154), dimensions={1}, to_apply=%bitcast.85.reduce_sub_computation | reduce | bytes 2097154
  20.3 7.5 %all-to-all-start = ((bf16[8,2,32768]{2,1,0:T(2,128)(2,1)}), bf16[8,2,32768]{2,1,0:T(2,128)(2,1)S(1)}, u32[]{:S(2)}, u32[]{:S(2)}) async-start(bf16[8,2,32768]{2,1,0:T(2,128)(2,1)} %reshape.206), calls=%async_computation | async-start | bytes 2097152 | tf_op jit(solution)/shard_map/all_to_all | solution.py:42
  32.9 13.0 %reduce.2 = bf16[8,131072]{1,0:T(8,128)(2,1)S(1)} reduce(bf16[8,1,131072]{2,1,0:T(2,128)(2,1)} %bitcast.100, bf16[]{:T(256)} %broadcast.154), dimensions={1}, to_apply=%bitcast.83.reduce_sub_computation | reduce | bytes 4194306
  49.1 4.4 all-to-all-done
  58.1 5.8 reshape.207
  77.6 28.9 %all-to-all-done.2 = bf16[8,2,65536]{2,1,0:T(2,128)(2,1)S(1)} async-done(((bf16[8,2,65536]{2,1,0:T(2,128)(2,1)}), bf16[8,2,65536]{2,1,0:T(2,128)(2,1)S(1)}, u32[]{:S(2)}, u32[]{:S(2)}) %all-to-all-start.2) | async-done | bytes 2097184 | tf_op jit(solution)/shard_map/all_to_all | solution.py:43
  106.5 4.7 all-to-all-start.1
  115.5 4.5 copy.79
  131.6 5.8 fusion.8
  137.3 5.0 all-to-all-start.3
  143.2 45.1 %copy.69 = bf16[1024,8,2,2048]{3,1,2,0:T(8,128)(2,1)} copy(bf16[1024,8,2,2048]{3,2,1,0:T(2,128)(2,1)} %bitcast.33) | data formatting | bytes 134217728
  188.3 83.4 %copy.48 = bf16[4096,8192]{1,0:T(8,128)(2,1)} copy(bf16[4096,8192]{0,1:T(8,128)(2,1)} %bitcast.1) | data formatting | bytes 134217728 | tf_op jit(solution)/shard_map/dot_general | solution.py:55
  274.9 5.4 gather_fusion.2
  280.3 7.9 %gather.27 = bf16[8,1024,256]{2,1,0:T(8,128)(2,1)} reshape(bf16[8,4,65536]{2,1,0:T(4,128)(2,1)} %gather_fusion.2) | data formatting | bytes 8388608 | tf_op jit(solution)/shard_map/jit(_take)/gather | solution.py:63
  288.3 5.2 copy.78
  294.5 5.4 gather_fusion.5
  299.9 5.5 gather_fusion.6
  305.4 8.3 %pad_maximum_fusion = bf16[8,4,131072]{2,1,0:T(4,128)(2,1)} fusion(bf16[8,4,65536]{2,1,0:T(4,128)(2,1)} %gather_fusion.6, bf16[8,4,65536]{2,1,0:T(4,128)(2,1)} %gather_fusion.5), kind=kLoop, calls=%fused_computation.15 | loop fusion | flops 16777216 | bytes 16777216
  313.8 12.5 %reshape.201 = bf16[8,4,128,2,512]{4,3,2,1,0:T(2,128)(2,1)} reshape(bf16[8,4,131072]{2,1,0:T(4,128)(2,1)} %pad_maximum_fusion) | data formatting | bytes 16777216 | tf_op jit(solution)/shard_map/jit(_take)/gather | solution.py:74
  326.3 8.2 %copy_select_fusion = bf16[8,4,128,2,512]{4,2,1,0,3:T(8,128)(2,1)} fusion(bf16[8,4,128,2,512]{4,3,2,1,0:T(2,128)(2,1)} %reshape.201, pred[8]{0:T(512)(128)(4,1)S(1)} %compare_and_fusion.1), kind=kLoop, calls=%fused_computation.16 | loop fusion | flops 4194304 | bytes 16777224 | tf_op jit(solution)/shard_map/jit(_take)/select_n | solution.py:74
  334.6 37.6 %all-gather.2.cloned.1.call-done = bf16[1024,8192]{1,0:T(8,128)(2,1)} async-done(((bf16[1024,1024]{1,0:T(8,128)(2,1)}), bf16[1024,8192]{1,0:T(8,128)(2,1)}) %all-gather.2.cloned.1.call-update) | async-done | bytes 16777232 | tf_op jit(solution)/shard_map/all_gather | solution.py:54
  372.2 10.3 %copy.70 = bf16[128,8,32,256]{3,2,1,0:T(8,128)(2,1)S(1)} copy(bf16[128,8,32,256]{3,1,2,0:T(8,128)(2,1)} %bitcast.102) | data formatting | bytes 33554432
  382.4 13.7 %dynamic-slice_reduce_fusion = bf16[1024,4,256]{2,1,0:T(4,128)(2,1)S(1)} fusion(bf16[1024,4,8,256]{3,2,1,0:T(8,128)(2,1)S(1)} %bitcast.98, s32[]{:T(128)S(6)} %select_n.80), kind=kLoop, calls=%fused_computation.27 | loop fusion | bytes 4194308 | tf_op jit(solution)/shard_map/dynamic_slice | solution.py:66
  402.6 70.0 %all-reduce.1 = bf16[8,128,256]{2,1,0:T(8,128)(2,1)S(1)} all-reduce(f32[8,128,256]{2,1,0:T(8,128)S(1)} %fusion.9), channel_id=1, replica_groups=mesh['grp'=4,'tp'=4,'cores'=2] {'tp','cores'}, use_global_device_ids=true, to_apply=%region_2.3 | all-reduce | flops 262144 | bytes 1572864 | tf_op jit(solution)/shard_map/psum | solution.py:73
  472.6 6.6 %broadcast_multiply_fusion.1 = f32[8,128,4,512]{3,1,2,0:T(8,128)} fusion(bf16[8,4,128,2,512]{4,2,1,0,3:T(8,128)(2,1)} %copy_select_fusion, bf16[8,128,256]{2,1,0:T(8,128)(2,1)S(1)} %all-reduce.1), kind=kOutput, calls=%fused_computation.24 | convolution fusion | flops 538968064 | bytes 12845056 | tf_op jit(solution)/shard_map/tkr,tmrw->tkmw/dot_general | solution.py:75
  479.2 6.6 %broadcast_multiply_fusion = f32[8,128,4,512]{3,1,2,0:T(8,128)} fusion(bf16[8,4,128,2,512]{4,2,1,0,3:T(8,128)(2,1)} %copy_select_fusion, bf16[8,128,256]{2,1,0:T(8,128)(2,1)S(1)} %all-reduce.1), kind=kOutput, calls=%fused_computation.23 | convolution fusion | flops 538968064 | bytes 12845056 | tf_op jit(solution)/shard_map/tkr,tmrw->tkmw/dot_general | solution.py:81
  485.8 12.1 %copy.60 = f32[8,128,4,512]{3,2,1,0:T(4,128)} copy(f32[8,128,4,512]{3,1,2,0:T(8,128)} %broadcast_multiply_fusion) | data formatting | bytes 16777216 | tf_op jit(solution)/shard_map/mul | solution.py:90
  497.9 11.1 %copy.72 = f32[128,8,4,512]{3,1,2,0:T(8,128)} copy(f32[128,8,4,512]{3,2,1,0:T(4,128)} %bitcast.94) | data formatting | bytes 16777216
  509.0 12.1 %copy.59 = f32[8,128,4,512]{3,2,1,0:T(4,128)} copy(f32[8,128,4,512]{3,1,2,0:T(8,128)} %broadcast_multiply_fusion.1) | data formatting | bytes 16777216 | tf_op jit(solution)/shard_map/mul | solution.py:87
  521.0 10.8 %copy.71 = f32[128,8,4,512]{3,1,2,0:T(8,128)} copy(f32[128,8,4,512]{3,2,1,0:T(4,128)} %bitcast.95) | data formatting | bytes 16777216
  531.8 80.5 %fusion = f32[1024,2,2048]{2,0,1:T(8,128)} fusion(bf16[2,2048,8192]{2,1,0:T(8,128)(2,1)} %bitcast.2, bf16[1024,8192]{1,0:T(8,128)(2,1)} %all-gather.2.cloned.1.call-done), kind=kOutput, calls=%fused_computation.7 | convolution fusion | flops 68719476736 | bytes 100663296 | tf_op jit(solution)/shard_map/dot_general | solution.py:55
  612.3 14.8 %fusion.4 = bf16[1024,2048]{1,0:T(8,128)(2,1)} fusion(f32[1024,2048]{1,0:T(8,128)} %bitcast.96, f32[1024,2,2048]{2,0,1:T(8,128)} %fusion, f32[1024,2048]{1,0:T(8,128)} %bitcast.97), kind=kLoop, calls=%fused_computation.12 | loop fusion | flops 16777216 | bytes 37748736 | tf_op jit(solution)/shard_map/convert_element_type | solution.py:93
  (49 shorter events, 60.6 us)
Async XLA Ops:
  6.5 21.4 %copy-start = (s32[8]{0:T(128)S(1)}, s32[8]{0:T(128)}, u32[]{:S(2)}) copy-start(s32[8]{0:T(128)} %param.13) | copy-start | bytes 100
  10.5 17.3 %copy-start.4 = (s32[4,3]{1,0:T(4,128)S(1)}, s32[4,3]{1,0:T(4,128)}, u32[]{:S(2)}) copy-start(s32[4,3]{1,0:T(4,128)} %param.11) | copy-start | bytes 148
  18.4 10.4 %copy-start.3 = (bf16[1,1,8,128,1024]{4,3,2,1,0:T(8,128)(2,1)S(1)}, bf16[1,1,8,128,1024]{4,3,2,1,0:T(8,128)(2,1)}, u32[]{:S(2)}) copy-start(bf16[1,1,8,128,1024]{4,3,2,1,0:T(8,128)(2,1)} %param.10) | copy-start | bytes 6291460
  20.3 33.2 %all-to-all-start = ((bf16[8,2,32768]{2,1,0:T(2,128)(2,1)}), bf16[8,2,32768]{2,1,0:T(2,128)(2,1)S(1)}, u32[]{:S(2)}, u32[]{:S(2)}) async-start(bf16[8,2,32768]{2,1,0:T(2,128)(2,1)} %reshape.206), calls=%async_computation | async-start | bytes 2097152 | tf_op jit(solution)/shard_map/all_to_all | solution.py:42
  53.5 1.0 copy-start.2
  54.5 52.0 %all-to-all-start.2 = ((bf16[8,2,65536]{2,1,0:T(2,128)(2,1)}), bf16[8,2,65536]{2,1,0:T(2,128)(2,1)S(1)}, u32[]{:S(2)}, u32[]{:S(2)}) async-start(bf16[8,2,65536]{2,1,0:T(2,128)(2,1)} %reshape.204), calls=%async_computation.2 | async-start | bytes 4194304 | tf_op jit(solution)/shard_map/all_to_all | solution.py:43
  106.5 30.8 %all-to-all-start.1 = ((bf16[4,3,1,65536]{3,1,2,0:T(4,128)(2,1)}), bf16[4,3,1,65536]{3,1,2,0:T(4,128)(2,1)}, u32[]{:S(2)}, u32[]{:S(2)}) async-start(bf16[4,3,1,65536]{3,1,2,0:T(4,128)(2,1)} %select_bitcast_fusion), calls=%async_computation.1 | async-start | bytes 4194304 | tf_op jit(solution)/shard_map/all_to_all | solution.py:49
  137.3 5.7 copy-start.5
  137.3 150.9 %all-to-all-start.3 = ((bf16[4,3,1,131072]{3,1,2,0:T(4,128)(2,1)}), bf16[4,3,1,131072]{3,1,2,0:T(4,128)(2,1)}, u32[]{:S(2)}, u32[]{:S(2)}) async-start(bf16[4,3,1,131072]{3,1,2,0:T(4,128)(2,1)} %fusion.8), calls=%async_computation.3 | async-start | bytes 8388608 | tf_op jit(solution)/shard_map/all_to_all | solution.py:50
  142.3 229.8 %all-gather.2.cloned.1.call-start = ((), (), s32[]{:S(2)}) async-start(), calls=%async_computation.4 | async-start | bytes 18874368 | tf_op jit(solution)/shard_map/all_gather | solution.py:54
  612.3 14.8 %copy-start.1 = (s32[8]{0:T(128)S(1)}, s32[8]{0:T(128)}, u32[]{:S(2)}) copy-start(s32[8]{0:T(128)} %param.13) | copy-start | bytes 100
Sparse Core Ops, SparseCore 0:
  145.3 226.8 all-gather.1
where the time goes:
time: 644 us; the launch traced here: 634 us
  local copies, waits for them, and re-layouts  299 us (46%)
  matrix products  97.5 us (15%)
  waiting for transfers between devices  71.2 us (11%)
  blocking collectives  70 us (11%)
  other arithmetic  61.6 us (10%)
  starting transfers between devices  21.2 us (3%)
  between operations  13.8 us (2%)
    unnamed x23, local copies, waits for them, and re-layouts  101 us
    dot_general x1, local copies, waits for them, and re-layouts, per_device(): jnp.dot(gathered, gate_up_weight.reshape(full_width, 2 * local_hidden_wid...  83.4 us
    dot_general x1, matrix products, per_device(): jnp.dot(gathered, gate_up_weight.reshape(full_width, 2 * local_hidden_wid...  80.5 us
    psum x1, blocking collectives, per_device(): lax.psum(partial_shrink, ('tp', 'cores')).astype(jnp.bfloat16)  70 us
    all_gather x1, waiting for transfers between devices, per_device(): gathered = lax.all_gather(tokens, ('tp', 'cores'), axis=1, tiled=True)  37.6 us
    all_to_all x1, waiting for transfers between devices, per_device(): lax.all_to_all(local_up_factor, ('tp', 'cores'), split_axis=1, concat_axi...  28.9 us
    unnamed x3, other arithmetic  28.6 us
    gather x4, local copies, waits for them, and re-layouts, per_device(): jnp.take(b_chosen, tile_seg, axis=0)  24.6 us
  transfers between devices with their start and end apart: 5, of which 3 were waited for; matrix products, arithmetic and copies ran while one was open for 41% of the time, Pallas kernels for 0%

commit v1 on v0

--- a/solution.py
+++ b/solution.py
@@ -5,6 +5,24 @@
 
 TILE = 128
 adapter_scale = 0.5
+
+
+def collect(value, axis, dim):
+    ways, here, step = (lax.axis_size(axis), lax.axis_index(axis), value.shape[dim])
+    shape = [n * ways if d == dim else n for d, n in enumerate(value.shape)]
+    full = lax.dynamic_update_slice_in_dim(
+        jnp.zeros(shape, value.dtype), value, here * step, axis=dim
+    )
+    going_up = going_down = value
+    for far in range(1, ways // 2 + 1):
+        going_up = lax.ppermute(going_up, axis, [(d, (d + 1) % ways) for d in range(ways)])
+        full = lax.dynamic_update_slice_in_dim(full, going_up, (here - far) % ways * step, axis=dim)
+        if 2 * far < ways:
+            going_down = lax.ppermute(going_down, axis, [(d, (d - 1) % ways) for d in range(ways)])
+            full = lax.dynamic_update_slice_in_dim(
+                full, going_down, (here + far) % ways * step, axis=dim
+            )
+    return full
 
 
 def tile_segments(tile_lengths, tile_count):
@@ -51,7 +69,7 @@
     )
     a_chosen = a_arrived.reshape(seg_count, groups, -1)
     b_chosen = b_arrived.reshape(seg_count, groups, -1)
-    gathered = lax.all_gather(tokens, ("tp", "cores"), axis=1, tiled=True)
+    gathered = collect(tokens, ("tp", "cores"), 1)
     frozen_output = jnp.dot(
         gathered,
         gate_up_weight.reshape(full_width, 2 * local_hidden_width),

time: 644 us -> 794 us (1.23)
  waiting for transfers between devices: 71.2 us -> 151 us
  starting transfers between devices: 21.2 us -> 80.7 us
  local copies, waits for them, and re-layouts: 299 us -> 325 us
  between operations: 13.8 us -> 0.51 us
    ppermute x0 -> x7, waiting for transfers between devices: none -> 102 us  [the longest x4 102 us: collect(): lax.ppermute(going_up, axis, [(d, (d + 1) % ways) for d in range(ways)])]
    all_to_all x1, starting transfers between devices: 3.6 us -> 46.2 us  [per_device(): lax.all_to_all(local_up_factor, ('tp', 'cores'), split_axis=1, concat_axi...]
    all_gather x1 -> x0, waiting for transfers between devices: 37.6 us -> none  [per_device(): gathered = lax.all_gather(tokens, ('tp', 'cores'), axis=1, tiled=True)]
    dynamic_update_slice x0 -> x8, local copies, waits for them, and re-layouts: none -> 21.5 us  [the longest x4 10.8 us: collect(): lax.dynamic_update_slice_in_dim(full, going_up, (here - far) % ways * ste...]
    all_to_all x1, waiting for transfers between devices: 28.9 us -> 48 us  [per_device(): lax.all_to_all(local_up_factor, ('tp', 'cores'), split_axis=1, concat_axi...]
    ppermute x0 -> x7, starting transfers between devices: none -> 17.4 us  [the longest x3 10.3 us: collect(): lax.ppermute(going_down, axis, [(d, (d - 1) % ways) for d in range(ways)])]
    unnamed x23 -> x29, local copies, waits for them, and re-layouts: 101 us -> 100 us
    unnamed x3 -> x4, other arithmetic: 28.6 us -> 28.5 us
  transfers between devices with their start and end apart: 5 -> 11, of which waited for: 3 -> 5; matrix products, arithmetic and copies ran while one was open for 41% -> 36% of each run, Pallas kernels for 0% -> 0%
where the time goes in v1:
time: 794 us; the launch traced here: 784 us
  local copies, waits for them, and re-layouts  325 us (41%)
  waiting for transfers between devices  151 us (19%)
  matrix products  97.8 us (12%)
  starting transfers between devices  80.7 us (10%)
  blocking collectives  69.8 us (9%)
  other arithmetic  59 us (7%)
    ppermute x4, waiting for transfers between devices, collect(): lax.ppermute(going_up, axis, [(d, (d + 1) % ways) for d in range(ways)])  102 us
    unnamed x29, local copies, waits for them, and re-layouts  100 us
    dot_general x1, local copies, waits for them, and re-layouts, per_device(): jnp.dot(gathered, gate_up_weight.reshape(full_width, 2 * local_hidden_wid...  83.3 us
    dot_general x1, matrix products, per_device(): jnp.dot(gathered, gate_up_weight.reshape(full_width, 2 * local_hidden_wid...  80.7 us
    psum x1, blocking collectives, per_device(): lax.psum(partial_shrink, ('tp', 'cores')).astype(jnp.bfloat16)  69.8 us
    all_to_all x1, waiting for transfers between devices, per_device(): lax.all_to_all(local_up_factor, ('tp', 'cores'), split_axis=1, concat_axi...  48 us
    all_to_all x1, starting transfers between devices, per_device(): lax.all_to_all(local_up_factor, ('tp', 'cores'), split_axis=1, concat_axi...  46.2 us
    unnamed x4, other arithmetic  28.5 us
  transfers between devices with their start and end apart: 11, of which 5 were waited for; matrix products, arithmetic and copies ran while one was open for 36% of the time, Pallas kernels for 0%

profile of v1, /device:TPU:0, one launch (start us, length us, event | category | flops | bytes accessed | tf_op | source)
XLA Modules:
  0.0 783.9 jit_solution(10731022973226848978)
XLA Ops:
  4.5 7.2 reduce.3
  13.6 7.3 all-to-all-start
  30.9 12.9 %reduce.2 = bf16[8,131072]{1,0:T(8,128)(2,1)S(1)} reduce(bf16[8,1,131072]{2,1,0:T(2,128)(2,1)} %bitcast.102, bf16[]{:T(256)} %broadcast.161), dimensions={1}, to_apply=%bitcast.83.reduce_sub_computation | reduce | bytes 4194306
  49.1 46.2 %all-to-all-start.2 = ((bf16[8,2,65536]{2,1,0:T(2,128)(2,1)}), bf16[8,2,65536]{2,1,0:T(2,128)(2,1)S(1)}, u32[]{:S(2)}, u32[]{:S(2)}) async-start(bf16[8,2,65536]{2,1,0:T(2,128)(2,1)} %reshape.204), calls=%async_computation.2 | async-start | bytes 4194304 | tf_op jit(solution)/shard_map/all_to_all | solution.py:61
  95.3 5.8 reshape.207
  114.9 25.4 %collective-permute-done = bf16[1024,1024]{1,0:T(8,128)(2,1)} collective-permute-done((bf16[1024,1024]{1,0:T(8,128)(2,1)}, bf16[1024,1024]{1,0:T(8,128)(2,1)}, u32[]{:S(2)}, u32[]{:S(2)}) %collective-permute-start) | collective-permute-done | bytes 2097184 | tf_op jit(solution)/shard_map/ppermute | solution.py:18
  145.0 48.0 %all-to-all-done.2 = bf16[8,2,65536]{2,1,0:T(2,128)(2,1)S(1)} async-done(((bf16[8,2,65536]{2,1,0:T(2,128)(2,1)}), bf16[8,2,65536]{2,1,0:T(2,128)(2,1)S(1)}, u32[]{:S(2)}, u32[]{:S(2)}) %all-to-all-start.2) | async-done | bytes 2097184 | tf_op jit(solution)/shard_map/all_to_all | solution.py:61
  218.0 5.8 fusion.8
  229.0 44.2 %copy.65 = bf16[1024,8,2,2048]{3,1,2,0:T(8,128)(2,1)} copy(bf16[1024,8,2,2048]{3,2,1,0:T(2,128)(2,1)} %bitcast.33) | data formatting | bytes 134217728
  273.3 83.3 %copy.46 = bf16[4096,8192]{1,0:T(8,128)(2,1)} copy(bf16[4096,8192]{0,1:T(8,128)(2,1)} %bitcast.1) | data formatting | bytes 134217728 | tf_op jit(solution)/shard_map/dot_general | solution.py:73
  356.9 6.0 broadcast_in_dim.49
  373.6 5.4 gather_fusion.2
  379.0 7.9 %gather.27 = bf16[8,1024,256]{2,1,0:T(8,128)(2,1)} reshape(bf16[8,4,65536]{2,1,0:T(4,128)(2,1)} %gather_fusion.2) | data formatting | bytes 8388608 | tf_op jit(solution)/shard_map/jit(_take)/gather | solution.py:81
  386.9 5.2 collective-permute-start.5
  404.5 5.4 gather_fusion.5
  409.9 5.4 gather_fusion.6
  415.3 62.8 %collective-permute-done.4 = bf16[1024,1024]{1,0:T(8,128)(2,1)} collective-permute-done((bf16[1024,1024]{1,0:T(8,128)(2,1)}, bf16[1024,1024]{1,0:T(8,128)(2,1)}, u32[]{:S(2)}, u32[]{:S(2)}) %collective-permute-start.4) | collective-permute-done | bytes 2097184 | tf_op jit(solution)/shard_map/ppermute | solution.py:18
  480.6 8.4 %pad_maximum_fusion = bf16[8,4,131072]{2,1,0:T(4,128)(2,1)} fusion(bf16[8,4,65536]{2,1,0:T(4,128)(2,1)} %gather_fusion.6, bf16[8,4,65536]{2,1,0:T(4,128)(2,1)} %gather_fusion.5), kind=kLoop, calls=%fused_computation.15 | loop fusion | flops 16777216 | bytes 16777216
  489.0 12.6 %reshape.201 = bf16[8,4,128,2,512]{4,3,2,1,0:T(2,128)(2,1)} reshape(bf16[8,4,131072]{2,1,0:T(4,128)(2,1)} %pad_maximum_fusion) | data formatting | bytes 16777216 | tf_op jit(solution)/shard_map/jit(_take)/gather | solution.py:92
  501.6 8.0 %copy_select_fusion = bf16[8,4,128,2,512]{4,2,1,0,3:T(8,128)(2,1)} fusion(bf16[8,4,128,2,512]{4,3,2,1,0:T(2,128)(2,1)} %reshape.201, pred[8]{0:T(512)(128)(4,1)S(1)} %compare_and_fusion.1), kind=kLoop, calls=%fused_computation.16 | loop fusion | flops 4194304 | bytes 16777224 | tf_op jit(solution)/shard_map/jit(_take)/select_n | solution.py:92
  515.8 13.6 %collective-permute-done.6 = bf16[1024,1024]{1,0:T(8,128)(2,1)S(1)} collective-permute-done((bf16[1024,1024]{1,0:T(8,128)(2,1)}, bf16[1024,1024]{1,0:T(8,128)(2,1)S(1)}, u32[]{:S(2)}, u32[]{:S(2)}) %collective-permute-start.6) | collective-permute-done | bytes 2097184 | tf_op jit(solution)/shard_map/ppermute | solution.py:18
  531.0 10.3 %copy.66 = bf16[128,8,32,256]{3,2,1,0:T(8,128)(2,1)S(1)} copy(bf16[128,8,32,256]{3,1,2,0:T(8,128)(2,1)} %bitcast.35) | data formatting | bytes 33554432
  541.2 13.7 %dynamic-slice_reduce_fusion = bf16[1024,4,256]{2,1,0:T(4,128)(2,1)S(1)} fusion(bf16[1024,4,8,256]{3,2,1,0:T(8,128)(2,1)S(1)} %bitcast.100, s32[]{:T(128)S(6)} %select_n.150), kind=kLoop, calls=%fused_computation.27 | loop fusion | bytes 4194308 | tf_op jit(solution)/shard_map/dynamic_slice | solution.py:84
  561.4 69.8 %all-reduce.1 = bf16[8,128,256]{2,1,0:T(8,128)(2,1)S(1)} all-reduce(f32[8,128,256]{2,1,0:T(8,128)S(1)} %fusion.9), channel_id=1, replica_groups=mesh['grp'=4,'tp'=4,'cores'=2] {'tp','cores'}, use_global_device_ids=true, to_apply=%region_2.3 | all-reduce | flops 262144 | bytes 1572864 | tf_op jit(solution)/shard_map/psum | solution.py:91
  631.2 6.6 broadcast_multiply_fusion.1
  637.8 6.7 broadcast_multiply_fusion
  644.6 80.7 %fusion = f32[1024,2,2048]{2,0,1:T(8,128)} fusion(bf16[2,2048,8192]{2,1,0:T(8,128)(2,1)} %bitcast.2, bf16[1024,8192]{1,0:T(8,128)(2,1)} %constant_dynamic-update-slice_fusion), kind=kOutput, calls=%fused_computation.7 | convolution fusion | flops 68719476736 | bytes 100663296 | tf_op jit(solution)/shard_map/dot_general | solution.py:73
  725.3 12.1 %copy.56 = f32[8,128,4,512]{3,2,1,0:T(4,128)} copy(f32[8,128,4,512]{3,1,2,0:T(8,128)} %broadcast_multiply_fusion.1) | data formatting | bytes 16777216 | tf_op jit(solution)/shard_map/mul | solution.py:105
  737.4 10.7 %copy.67 = f32[128,8,4,512]{3,1,2,0:T(8,128)} copy(f32[128,8,4,512]{3,2,1,0:T(4,128)} %bitcast.94) | data formatting | bytes 16777216
  748.1 12.2 %copy.57 = f32[8,128,4,512]{3,2,1,0:T(4,128)} copy(f32[8,128,4,512]{3,1,2,0:T(8,128)} %broadcast_multiply_fusion) | data formatting | bytes 16777216 | tf_op jit(solution)/shard_map/mul | solution.py:108
  760.3 10.9 %copy.68 = f32[128,8,4,512]{3,1,2,0:T(8,128)} copy(f32[128,8,4,512]{3,2,1,0:T(4,128)} %bitcast.95) | data formatting | bytes 16777216
  771.3 12.5 %fusion.4 = bf16[1024,2048]{1,0:T(8,128)(2,1)} fusion(f32[1024,2048]{1,0:T(8,128)} %bitcast.99, f32[1024,2,2048]{2,0,1:T(8,128)} %fusion, f32[1024,2048]{1,0:T(8,128)S(1)} %bitcast.98), kind=kLoop, calls=%fused_computation.12 | loop fusion | flops 16777216 | bytes 37748736 | tf_op jit(solution)/shard_map/convert_element_type | solution.py:111
  (76 shorter events, 110.5 us)
Async XLA Ops:
  0.0 25.9 %copy-start = (s32[8]{0:T(128)S(1)}, s32[8]{0:T(128)}, u32[]{:S(2)}) copy-start(s32[8]{0:T(128)} %param.13) | copy-start | bytes 100
  4.0 21.8 %copy-start.5 = (s32[4,3]{1,0:T(4,128)S(1)}, s32[4,3]{1,0:T(4,128)}, u32[]{:S(2)}) copy-start(s32[4,3]{1,0:T(4,128)} %param.11) | copy-start | bytes 148
  11.7 15.0 %copy-start.3 = (bf16[1,1,8,128,1024]{4,3,2,1,0:T(8,128)(2,1)S(1)}, bf16[1,1,8,128,1024]{4,3,2,1,0:T(8,128)(2,1)}, u32[]{:S(2)}) copy-start(bf16[1,1,8,128,1024]{4,3,2,1,0:T(8,128)(2,1)} %param.10) | copy-start | bytes 6291460
  13.6 34.5 %all-to-all-start = ((bf16[8,2,32768]{2,1,0:T(2,128)(2,1)}), bf16[8,2,32768]{2,1,0:T(2,128)(2,1)S(1)}, u32[]{:S(2)}, u32[]{:S(2)}) async-start(bf16[8,2,32768]{2,1,0:T(2,128)(2,1)} %reshape.206), calls=%async_computation | async-start | bytes 2097152 | tf_op jit(solution)/shard_map/all_to_all | solution.py:60
  20.9 119.4 %collective-permute-start = (bf16[1024,1024]{1,0:T(8,128)(2,1)}, bf16[1024,1024]{1,0:T(8,128)(2,1)}, u32[]{:S(2)}, u32[]{:S(2)}) collective-permute-start(bf16[1024,1024]{1,0:T(8,128)(2,1)} %param.7), channel_id=1, source_target_pairs={{0,1},{1,2},{2,3},{3,4},{4,5},{5,6},{6,7},{7,0},{8,9},{9,10},{10,1... | collective-permute-start | bytes 6291464 | tf_op jit(solution)/shard_map/ppermute | solution.py:18
  22.9 119.8 %collective-permute-start.1 = (bf16[1024,1024]{1,0:T(8,128)(2,1)}, bf16[1024,1024]{1,0:T(8,128)(2,1)}, u32[]{:S(2)}, u32[]{:S(2)}) collective-permute-start(bf16[1024,1024]{1,0:T(8,128)(2,1)} %param.7), channel_id=1, source_target_pairs={{0,7},{1,0},{2,1},{3,2},{4,3},{5,4},{6,5},{7,6},{8,15},{9,8},{10,9... | collective-permute-start | bytes 6291464 | tf_op jit(solution)/shard_map/ppermute | solution.py:21
  48.1 1.0 copy-start.2
  49.1 143.9 %all-to-all-start.2 = ((bf16[8,2,65536]{2,1,0:T(2,128)(2,1)}), bf16[8,2,65536]{2,1,0:T(2,128)(2,1)S(1)}, u32[]{:S(2)}, u32[]{:S(2)}) async-start(bf16[8,2,65536]{2,1,0:T(2,128)(2,1)} %reshape.204), calls=%async_computation.2 | async-start | bytes 4194304 | tf_op jit(solution)/shard_map/all_to_all | solution.py:61
  140.3 246.6 %collective-permute-start.2 = (bf16[1024,1024]{1,0:T(8,128)(2,1)}, bf16[1024,1024]{1,0:T(8,128)(2,1)}, u32[]{:S(2)}, u32[]{:S(2)}) collective-permute-start(bf16[1024,1024]{1,0:T(8,128)(2,1)} %collective-permute-done), channel_id=1, source_target_pairs={{0,1},{1,2},{2,3},{3,4},{4,5},{5,6},{6,7},{7,0},{8,9},{9,10},{10,1... | collective-permute-start | bytes 6291464 | tf_op jit(solution)/shard_map/ppermute | solution.py:18
  142.8 244.2 %collective-permute-start.3 = (bf16[1024,1024]{1,0:T(8,128)(2,1)}, bf16[1024,1024]{1,0:T(8,128)(2,1)}, u32[]{:S(2)}, u32[]{:S(2)}) collective-permute-start(bf16[1024,1024]{1,0:T(8,128)(2,1)} %collective-permute-done.1), channel_id=1, source_target_pairs={{0,7},{1,0},{2,1},{3,2},{4,3},{5,4},{6,5},{7,6},{8,15},{9,8},{10,9... | collective-permute-start | bytes 6291464 | tf_op jit(solution)/shard_map/ppermute | solution.py:21
  193.0 30.8 %all-to-all-start.1 = ((bf16[4,3,1,65536]{3,1,2,0:T(4,128)(2,1)}), bf16[4,3,1,65536]{3,1,2,0:T(4,128)(2,1)}, u32[]{:S(2)}, u32[]{:S(2)}) async-start(bf16[4,3,1,65536]{3,1,2,0:T(4,128)(2,1)} %select_bitcast_fusion), calls=%async_computation.1 | async-start | bytes 4194304 | tf_op jit(solution)/shard_map/all_to_all | solution.py:67
  223.8 174.4 %all-to-all-start.3 = ((bf16[4,3,1,131072]{3,1,2,0:T(4,128)(2,1)}), bf16[4,3,1,131072]{3,1,2,0:T(4,128)(2,1)}, u32[]{:S(2)}, u32[]{:S(2)}) async-start(bf16[4,3,1,131072]{3,1,2,0:T(4,128)(2,1)} %fusion.8), calls=%async_computation.3 | async-start | bytes 8388608 | tf_op jit(solution)/shard_map/all_to_all | solution.py:68
  273.3 83.3 %copy-start.6 = (s32[1,3]{1,0:T(1,128)S(1)}, s32[1,3]{1,0:T(1,128)}, u32[]{:S(2)}) copy-start(s32[1,3]{1,0:T(1,128)} %param.12) | copy-start | bytes 40
  356.9 6.0 copy-start.4
  386.9 91.1 %collective-permute-start.4 = (bf16[1024,1024]{1,0:T(8,128)(2,1)}, bf16[1024,1024]{1,0:T(8,128)(2,1)}, u32[]{:S(2)}, u32[]{:S(2)}) collective-permute-start(bf16[1024,1024]{1,0:T(8,128)(2,1)} %collective-permute-done.2), channel_id=1, source_target_pairs={{0,1},{1,2},{2,3},{3,4},{4,5},{5,6},{6,7},{7,0},{8,9},{9,10},{10,1... | collective-permute-start | bytes 6291464 | tf_op jit(solution)/shard_map/ppermute | solution.py:18
  386.9 125.8 %collective-permute-start.5 = (bf16[1024,1024]{1,0:T(8,128)(2,1)}, bf16[1024,1024]{1,0:T(8,128)(2,1)}, u32[]{:S(2)}, u32[]{:S(2)}) collective-permute-start(bf16[1024,1024]{1,0:T(8,128)(2,1)} %collective-permute-done.3), channel_id=1, source_target_pairs={{0,7},{1,0},{2,1},{3,2},{4,3},{5,4},{6,5},{7,6},{8,15},{9,8},{10,9... | collective-permute-start | bytes 6291464 | tf_op jit(solution)/shard_map/ppermute | solution.py:21
  478.0 51.4 %collective-permute-start.6 = (bf16[1024,1024]{1,0:T(8,128)(2,1)}, bf16[1024,1024]{1,0:T(8,128)(2,1)S(1)}, u32[]{:S(2)}, u32[]{:S(2)}) collective-permute-start(bf16[1024,1024]{1,0:T(8,128)(2,1)} %collective-permute-done.4), channel_id=1, source_target_pairs={{0,1},{1,2},{2,3},{3,4},{4,5},{5,6},{6,7},{7,0},{8,9},{9,10},{10,1... | collective-permute-start | bytes 6291464 | tf_op jit(solution)/shard_map/ppermute | solution.py:18
  760.3 11.0 %slice-start = ((s8[8388608]{0:T(1024)(128)(4,1)}), s8[4194304]{0:T(1024)(128)(4,1)S(1)}, s32[]{:S(2)}) async-start(s8[8388608]{0:T(1024)(128)(4,1)} %bitcast.96), calls=%async_computation.4 | async-start | bytes 8388608
  760.3 11.0 %slice-start.1 = ((s8[8388608]{0:T(1024)(128)(4,1)}), s8[4194304]{0:T(1024)(128)(4,1)S(1)}, s32[]{:S(2)}) async-start(s8[8388608]{0:T(1024)(128)(4,1)} %bitcast.96), calls=%async_computation.5 | async-start | bytes 8388608
  771.3 12.5 %copy-start.1 = (s32[8]{0:T(128)S(1)}, s32[8]{0:T(128)}, u32[]{:S(2)}) copy-start(s32[8]{0:T(128)} %param.13) | copy-start | bytes 100
